TPU v7x, 512 devices: a whole 4x4x16 slice. The times are simulated.
512 devices in a mesh: section: 32 (over y, x, core), ctx: 16 (over z).
Axes of the slice: x: 4, y: 4, z: 16, core: 2. Of those that a mesh axis runs over, the one named last changes fastest.
Arguments:
- streams: bfloat16 [32, 2048, 5120], P('section', 'ctx'), may hold values from -6 to 6
- conv_weight: bfloat16 [32, 4, 5120], P('section'), may hold values from -3 to 3
- beta_logit: float32 [32, 2048, 16], P('section', 'ctx'), may hold values from -12 to 3
- gate_log: float32 [32, 2048, 8], P('section', 'ctx'), may hold values from -2 to 0
- norm_gain: float32 [32, 1024], P('section'), may hold values from 0.25 to 1.75
- w_out: bfloat16 [32, 1024, 2048], P('section', None, 'ctx'), may hold values from -0.1875 to 0.1875
Outputs:
- handed: bfloat16 [32, 2048, 2048], P('section', 'ctx')
All inputs are finite; a program needn't handle non-finite values.
Results may differ from a plain program's by a relative error of at most 0.0049.
Values may be sent and summed in bfloat16 or wider, within the bound.
A program may use at most 128 MiB of HBM per device.

v0:
```python
import jax
import jax.numpy as jnp
from jax import lax
from jax.sharding import PartitionSpec as P

HEAD_TOTAL = 8
HK = 128
STEPS = 2
CONV = 4
SPAN = 128
highest = lax.Precision.HIGHEST


def shifted(value, axis, steps):
    count = lax.axis_size(axis)
    first, last = (max(0, -steps), min(count, count - steps))
    return lax.ppermute(value, axis, [(source, source + steps) for source in range(first, last)])


def entering(value, axis, join, neutral):
    count, mine = (lax.axis_size(axis), lax.axis_index(axis))
    pieces = jax.tree.map(lambda part: lax.all_gather(part, axis), value)
    total = jax.tree.map(
        lambda part, zero: jnp.full_like(part, 0) + jnp.asarray(zero, part.dtype), value, neutral
    )

    def turn(position, total):
        longer = join(total, jax.tree.map(lambda part: part[position], pieces))
        return jax.tree.map(lambda new, old: jnp.where(position < mine, new, old), longer, total)

    return lax.fori_loop(0, count - 1, turn, total)


def passed_along(value, axis, steps):
    count = lax.axis_size(axis)
    pairs = [(source, (source + steps) % count) for source in range(count)]
    return lax.ppermute(value, axis, pairs)


def mix_taps(extended, tap_weights):
    tok_count = extended.shape[0] - tap_weights.shape[0] + 1
    summed = jnp.zeros((tok_count, extended.shape[1]), jnp.float32)
    for offset in range(tap_weights.shape[0]):
        summed = summed + tap_weights[offset].astype(jnp.float32) * extended[
            offset : offset + tok_count
        ].astype(jnp.float32)
    return jax.nn.silu(summed)


def unit_rows(vectors):
    return vectors * lax.rsqrt(jnp.sum(vectors * vectors, axis=-1, keepdims=True) + 1e-06)


def head_major(active, beta_logit, gate_log):
    tok_count = active.shape[0]
    head_width = HEAD_TOTAL * HK
    queries = unit_rows(active[:, :head_width].reshape(tok_count, HEAD_TOTAL, HK)).transpose(
        1, 0, 2
    )
    keys_all = unit_rows(
        active[:, head_width : (1 + STEPS) * head_width].reshape(tok_count, STEPS, HEAD_TOTAL, HK)
    )
    keys_all = keys_all.transpose(2, 0, 1, 3).reshape(HEAD_TOTAL, tok_count * STEPS, HK)
    values_all = active[:, (1 + STEPS) * head_width :].reshape(tok_count, STEPS, HEAD_TOTAL, HK)
    values_all = values_all.transpose(2, 0, 1, 3).reshape(HEAD_TOTAL, tok_count * STEPS, HK)
    step_size = (
        jax.nn.sigmoid(beta_logit.reshape(tok_count, STEPS, HEAD_TOTAL))
        .transpose(2, 0, 1)
        .reshape(HEAD_TOTAL, tok_count * STEPS)
    )
    opening = (lax.broadcasted_iota(jnp.int32, (1, STEPS, 1), 1) == 0).astype(gate_log.dtype)
    log_gate = (
        (gate_log[:, None, :] * opening).transpose(2, 0, 1).reshape(HEAD_TOTAL, tok_count * STEPS)
    )
    return (queries, keys_all, values_all, step_size, log_gate)


def span_terms(queries, keys_all, values_all, step_size, log_gate):
    head_count, virtual, head_dim = keys_all.shape
    blocks = virtual // SPAN
    per_block = SPAN // STEPS
    queries = queries.reshape(head_count, blocks, per_block, head_dim)
    keys_all = keys_all.reshape(head_count, blocks, SPAN, head_dim)
    values_all = values_all.reshape(head_count, blocks, SPAN, head_dim)
    step_size = step_size.reshape(head_count, blocks, SPAN)
    cumulate = jnp.cumsum(log_gate.reshape(head_count, blocks, SPAN), axis=-1)
    query_log = cumulate[..., STEPS - 1 :: STEPS]
    row_index = lax.broadcasted_iota(jnp.int32, (SPAN, SPAN), 0)
    col_index = lax.broadcasted_iota(jnp.int32, (SPAN, SPAN), 1)
    strict = col_index < row_index
    spread = cumulate[..., :, None] - cumulate[..., None, :]
    damping = jnp.where(strict, jnp.exp(jnp.where(strict, spread, 0.0)), 0.0)
    key_inner = jnp.einsum("hcid,hcjd->hcij", keys_all, keys_all, precision=highest)
    unit_lower = (
        jnp.eye(SPAN, dtype=key_inner.dtype) + step_size[..., :, None] * damping * key_inner
    )
    right_sides = jnp.concatenate(
        [step_size[..., None] * values_all, (step_size * jnp.exp(cumulate))[..., None] * keys_all],
        axis=-1,
    )
    solved = jax.scipy.linalg.solve_triangular(
        unit_lower, right_sides, lower=True, unit_diagonal=True
    )
    value_part = solved[..., :head_dim]
    key_part = solved[..., head_dim:]
    to_end = keys_all * jnp.exp(cumulate[..., -1:] - cumulate)[..., None]
    carried = jnp.exp(cumulate[..., -1])[..., None, None] * jnp.eye(head_dim, dtype=key_inner.dtype)
    carried = carried - jnp.einsum("hcid,hcie->hcde", to_end, key_part, precision=highest)
    written = jnp.einsum("hcid,hcie->hcde", to_end, value_part, precision=highest)
    query_row = lax.broadcasted_iota(jnp.int32, (per_block, SPAN), 0) * STEPS + STEPS - 1
    query_col = lax.broadcasted_iota(jnp.int32, (per_block, SPAN), 1)
    allowed = query_col <= query_row
    query_spread = query_log[..., :, None] - cumulate[..., None, :]
    query_damping = jnp.where(allowed, jnp.exp(jnp.where(allowed, query_spread, 0.0)), 0.0)
    scores = jnp.einsum("hcpd,hcid->hcpi", queries, keys_all, precision=highest) * query_damping
    direct = jnp.einsum("hcpi,hcie->hcpe", scores, value_part, precision=highest)
    reach_map = queries * jnp.exp(query_log)[..., None] - jnp.einsum(
        "hcpi,hcie->hcpe", scores, key_part, precision=highest
    )
    return (
        jnp.moveaxis(carried, 1, 0),
        jnp.moveaxis(written, 1, 0),
        jnp.moveaxis(direct, 1, 0),
        jnp.moveaxis(reach_map, 1, 0),
    )


def advance(state_now, piece_terms):
    carried, written, direct, reach_map = piece_terms
    span_out = direct + jnp.einsum("hpd,hde->hpe", reach_map, state_now, precision=highest)
    state_now = jnp.einsum("hde,hef->hdf", carried, state_now, precision=highest) + written
    return (state_now, span_out)


def normalize(outputs, norm_gain):
    tok_count = outputs.shape[0]
    inverse_rms = lax.rsqrt(jnp.mean(outputs * outputs, axis=-1, keepdims=True) + 1e-05)
    return (
        (outputs * inverse_rms * norm_gain.reshape(HEAD_TOTAL, HK))
        .reshape(tok_count, HEAD_TOTAL * HK)
        .astype(jnp.bfloat16)
    )


def combine_pairs(earlier_pair, later_pair):
    first_map, first_add = earlier_pair
    second_map, second_add = later_pair
    joined_map = jnp.einsum("hde,hef->hdf", second_map, first_map, precision=highest)
    joined_add = jnp.einsum("hde,hef->hdf", second_map, first_add, precision=highest) + second_add
    return (joined_map, joined_add)


def compose_step(carried_in, piece_terms):
    so_far, added_state = carried_in
    next_map = jnp.einsum("hde,hef->hdf", piece_terms[0], so_far, precision=highest)
    next_add = (
        jnp.einsum("hde,hef->hdf", piece_terms[0], added_state, precision=highest) + piece_terms[1]
    )
    return ((next_map, next_add), None)


def on_device(streams, conv_weight, beta_logit, gate_log, norm_gain, w_out):
    own_rows = streams[0]
    tok_count = own_rows.shape[0]
    rim_rows = shifted(own_rows[tok_count - (CONV - 1) :], "ctx", 1)
    active = mix_taps(jnp.concatenate([rim_rows, own_rows], axis=0), conv_weight[0])
    span_parts = span_terms(*head_major(active, beta_logit[0], gate_log[0]))
    identity_map = jnp.broadcast_to(jnp.eye(HK, dtype=jnp.float32), (HEAD_TOTAL, HK, HK))
    nothing = jnp.zeros((HEAD_TOTAL, HK, HK), jnp.float32)
    (total_map, total_add), _ = lax.scan(compose_step, (identity_map, nothing), span_parts)
    _, incoming = entering((total_map, total_add), "ctx", combine_pairs, (identity_map, nothing))
    _, outputs = lax.scan(advance, incoming, span_parts)
    outputs = outputs.transpose(0, 2, 1, 3).reshape(tok_count, HEAD_TOTAL, HK)
    normed = normalize(outputs, norm_gain[0])
    local_cols = w_out[0]
    mixed_rows = jnp.dot(
        normed,
        lax.all_gather(local_cols, "ctx", axis=1, tiled=True),
        preferred_element_type=jnp.float32,
    ).astype(jnp.bfloat16)
    return passed_along(mixed_rows[None], "section", 1)


def solution(mesh):
    placed = (
        P("section", "ctx", None),
        P("section", None, None),
        P("section", "ctx", None),
        P("section", "ctx", None),
        P("section", None),
        P("section", None, "ctx"),
    )
    return jax.shard_map(
        on_device, mesh=mesh, in_specs=placed, out_specs=P("section", "ctx", None), check_vma=False
    )
```

profile of v0, /device:TPU:32, one launch (start us, length us, event | category | flops | bytes accessed | tf_op | source)
XLA Modules:
  0.0 527.9 jit_solution(1281271470755481892)
XLA Ops:
  6.5 1.0 slice_bitcast_fusion.3
  7.6 3.8 collective-permute-start
  11.4 1.0 slice_convert_fusion.3
  12.4 0.8 copy.80
  14.3 0.7 divide_bitcast_fusion
  16.3 1.8 divide_multiply_fusion
  18.5 1.1 copy-done.6
  21.2 1.5 copy.89
  22.7 2.4 fusion.43
  25.1 157.9 %custom-call.4 = f32[8,2,1,128,128]{3,4,2,1,0:T(8,128)} custom-call(f32[8,2,1,128,128]{4,3,2,1,0:T(8,128)S(1)} %fusion.43), custom_call_target="InvertDiagBlocksLowerTriangular" | custom-call | tf_op jit(solution)/shard_map/jit(_solve_triangular)/vmap(vmap())/triangular_solve | solution.py:101
  183.0 1.9 broadcast_multiply_fusion
  184.9 2.0 fusion.35
  186.9 2.2 convolution_bitcast_fusion
  189.3 2.2 fusion.39
  191.7 2.9 while.40
  194.6 0.8 copy-done.2
  197.2 1.2 slice_bitcast_fusion.2
  199.0 2.1 convolution_multiply_fusion.1
  201.2 1.9 convolution_bitcast_fusion.2
  203.0 1.1 fusion.46
  204.1 97.6 %all-gather.7.cloned.1.call-done = f32[128,128,128]{2,1,0:T(8,128)} async-done(((f32[8,128,128]{2,1,0:T(8,128)}), f32[128,128,128]{2,1,0:T(8,128)}) %all-gather.7.cloned.1.call-update) | async-done | bytes 8388624 | tf_op jit(solution)/shard_map/all_gather | solution.py:22
  301.7 105.9 %all-gather.9.cloned.1.call-done = f32[128,128,128]{2,1,0:T(8,128)} async-done(((f32[8,128,128]{2,1,0:T(8,128)}), f32[128,128,128]{2,1,0:T(8,128)}) %all-gather.9.cloned.1.call-update) | async-done | bytes 8388624 | tf_op jit(solution)/shard_map/all_gather | solution.py:22
  407.6 29.2 %while.41 = (s32[]{:T(128)}, f32[8,128,128]{2,1,0:T(8,128)S(1)}, s32[]{:T(128)}, f32[16,8,128,128]{3,2,1,0:T(8,128)}, f32[16,8,128,128]{3,2,1,0:T(8,128)}, /*index=5*/s32[]{:T(128)}, s32[]{:T(128)}) while((s32[]{:T(128)}, f32[8,128,128]{2,1,0:T(8,128)S(1)}, s32[]{:T(128)}, f32[16,8,128,128]{3,2,1,0:T(8,128)}, ...), condition=%wide.region_5.6_spmd.clone, body=%wide.region_4.5_spmd.clone.sunk | while | flops 201850880 | bytes 3672671 | solution.py:31
  407.6 1.9 fusion.97
  409.6 1.9 fusion.97
  411.5 1.9 fusion.97
  413.5 1.9 fusion.97
  415.4 1.9 fusion.97
  417.4 1.9 fusion.97
  419.3 1.9 fusion.97
  421.3 1.9 fusion.97
  423.2 1.9 fusion.97
  425.2 1.9 fusion.97
  427.1 1.9 fusion.97
  429.1 1.9 fusion.97
  431.0 1.9 fusion.97
  433.0 1.9 fusion.97
  434.9 1.9 fusion.97
  436.8 6.0 %while.39 = (s32[]{:T(128)}, f32[8,128,128]{2,1,0:T(8,128)S(1)}, f32[2,8,64,128]{3,2,1,0:T(8,128)}, f32[2,8,128,128]{3,2,1,0:T(8,128)S(1)}, f32[2,8,128,128]{3,2...) while((s32[]{:T(128)}, f32[8,128,128]{2,1,0:T(8,128)S(1)}, ...), condition=%wide.region_8.9_spmd, body=%wide.region_7.8_spmd.sunk | while | flops 302186496 | bytes 4458581 | solution.py:172
  436.9 2.3 fusion.89
  439.9 2.3 fusion.89
  442.8 1.3 multiply_reduce_fusion.1
  444.2 1.4 copy.105
  445.5 58.0 %all-gather.11.cloned.1.call-done = bf16[1,1024,2048]{2,1,0:T(8,128)(2,1)} async-done(((bf16[1,1024,128]{2,1,0:T(8,128)(2,1)}), bf16[1,1024,2048]{2,1,0:T(8,128)(2,1)}) %all-gather.11.cloned.1.call-update) | async-done | bytes 4194320 | tf_op jit(solution)/shard_map/all_gather | solution.py:178
  503.7 3.0 fusion.32
  506.7 1.9 collective-permute-start.1
  508.7 11.9 %collective-permute-done.1 = bf16[1,128,2048]{2,1,0:T(8,128)(2,1)S(1)} collective-permute-done((bf16[1,128,2048]{2,1,0:T(8,128)(2,1)S(1)}, bf16[1,128,2048]{2,1,0:T(8,128)(2,1)S(1)}, u32[]{:S(2)}, u32[]{:S(2)}) %collective-permute-start.1) | collective-permute-done | bytes 524320 | tf_op jit(solution)/shard_map/ppermute | solution.py:37
  520.5 0.8 copy.160
  (99 shorter events, 11.8 us)
Async XLA Ops:
  6.5 9.7 %copy-start.7 = (bf16[1,128,5120]{2,1,0:T(8,128)(2,1)S(1)}, bf16[1,128,5120]{2,1,0:T(8,128)(2,1)}, u32[]{:S(2)}) copy-start(bf16[1,128,5120]{2,1,0:T(8,128)(2,1)} %param.12) | copy-start | bytes 3932164
  6.5 295.1 %all-gather.7.cloned.1.call-start = ((), (), s32[]{:S(2)}) async-start(), calls=%async_computation | async-start | bytes 8912896 | tf_op jit(solution)/shard_map/all_gather | solution.py:22
  7.6 8.7 %collective-permute-start = (bf16[3,5120]{1,0:T(4,128)(2,1)S(1)}, bf16[3,5120]{1,0:T(4,128)(2,1)S(1)}, u32[]{:S(2)}, u32[]{:S(2)}) collective-permute-start(bf16[3,5120]{1,0:T(4,128)(2,1)S(1)} %slice_bitcast_fusion.3), channel_id=1, source_target_pairs={{0,1},{1,2},{2,3},{3,4},{4,5},{5,6},{6,7},{7,8},{8,9},{9,10},{10,1... | collective-permute-start | bytes 92168 | tf_op jit(solution)/shard_map/ppermute | solution.py:17
  18.1 1.5 copy-start.6
  21.0 168.3 %copy-start = (f32[8,128,2,128]{3,2,1,0:T(2,128)}, f32[8,128,2,128]{3,2,1,0:T(2,128)S(1)}, u32[]{:S(2)}) copy-start(f32[8,128,2,128]{3,2,1,0:T(2,128)S(1)} %copy.83) | copy-start | bytes 3145732
  183.0 1.9 copy-start.8
  186.9 2.3 copy-start.3
  194.5 0.8 copy-start.2
  194.5 1.0 copy-start.5
  195.4 212.2 %all-gather.9.cloned.1.call-start = ((), (), s32[]{:S(2)}) async-start(), calls=%async_computation.1 | async-start | bytes 8912896 | tf_op jit(solution)/shard_map/all_gather | solution.py:22
  196.1 307.4 %all-gather.11.cloned.1.call-start = ((), (), s32[]{:S(2)}) async-start(), calls=%async_computation.2 | async-start | bytes 4456448 | tf_op jit(solution)/shard_map/all_gather | solution.py:178
  197.1 1.9 copy-start.1
  198.5 2.7 copy-start.4
  436.8 66.9 %copy-start.9 = (f32[1,1024]{1,0:T(1,128)S(1)}, f32[1,1024]{1,0:T(1,128)}, u32[]{:S(2)}) copy-start(f32[1,1024]{1,0:T(1,128)} %param.16) | copy-start | bytes 12292
  506.7 13.8 %collective-permute-start.1 = (bf16[1,128,2048]{2,1,0:T(8,128)(2,1)S(1)}, bf16[1,128,2048]{2,1,0:T(8,128)(2,1)S(1)}, u32[]{:S(2)}, u32[]{:S(2)}) collective-permute-start(bf16[1,128,2048]{2,1,0:T(8,128)(2,1)S(1)} %fusion.32), channel_id=1, source_target_pairs={{0,16},{16,32},{32,48},{48,64},{64,80},{80,96},{96,112},{112,128},... | collective-permute-start | bytes 1572872 | tf_op jit(solution)/shard_map/ppermute | solution.py:37
Sparse Core Ops, SparseCore 0:
  195.5 106.1 all-gather.6
  303.8 103.7 all-gather.8
  409.6 93.8 all-gather.10
where the time goes:
time: 529 us; the launch traced here: 528 us
  waiting for transfers between devices  275 us (52%)
  other arithmetic  167 us (32%)
  matrix products  53.5 us (10%)
  between operations  13.6 us (3%)
  local copies, waits for them, and re-layouts  12.2 us (2%)
  starting transfers between devices  6.05 us (1%)
    all_gather x2, waiting for transfers between devices, entering(): pieces = jax.tree.map(lambda part: lax.all_gather(part, axis), value)  203 us
    another operation x2, other arithmetic, span_terms(): jax.scipy.linalg.solve_triangular(unit_lower, right_sides, lower=True, un...  158 us
    all_gather x1, waiting for transfers between devices, on_device(): lax.all_gather(local_cols, 'ctx', axis=1, tiled=True)  58 us
    dot_general x15, matrix products, combine_pairs(): jnp.einsum('hde,hef->hdf', second_map, first_add, precision=highest)  28.1 us
    ppermute x1, waiting for transfers between devices, passed_along(): return lax.ppermute(value, axis, pairs)  11.9 us
  transfers between devices with their start and end apart: 5, of which 5 were waited for; matrix products, arithmetic and copies ran while one was open for 9% of the time, Pallas kernels for 0%

commit v1 on v0

--- a/solution.py
+++ b/solution.py
@@ -9,6 +9,33 @@
 CONV = 4
 SPAN = 128
 highest = lax.Precision.HIGHEST
+
+
+def time_the_levels_all(point, which_dim):
+    dev_axis = "ctx"
+    n_now = lax.axis_size(dev_axis)
+    everything = lax.axis_index(dev_axis)
+    val2, item_now, mat_out = (n_now, everything, point.shape[which_dim])
+    series = [tick * val2 if dev_j == which_dim else tick for dev_j, tick in enumerate(point.shape)]
+    u_next = lax.dynamic_update_slice_in_dim(
+        jnp.zeros(series, point.dtype), point, item_now * mat_out, axis=which_dim
+    )
+    taken_in = e_next = point
+    for num in [*range(1, val2 // 2 + 1)]:
+        taken_in = lax.ppermute(
+            taken_in, dev_axis, [(dev_j, (dev_j + 1) % val2) for dev_j in range(val2)]
+        )
+        u_next = lax.dynamic_update_slice_in_dim(
+            u_next, taken_in, (item_now - num) % val2 * mat_out, axis=which_dim
+        )
+        if 2 * num < val2:
+            e_next = lax.ppermute(
+                e_next, dev_axis, [(dev_j, (dev_j - 1) % val2) for dev_j in range(val2)]
+            )
+            u_next = lax.dynamic_update_slice_in_dim(
+                u_next, e_next, (item_now + num) % val2 * mat_out, axis=which_dim
+            )
+    return u_next
 
 
 def shifted(value, axis, steps):
@@ -174,9 +201,7 @@
     normed = normalize(outputs, norm_gain[0])
     local_cols = w_out[0]
     mixed_rows = jnp.dot(
-        normed,
-        lax.all_gather(local_cols, "ctx", axis=1, tiled=True),
-        preferred_element_type=jnp.float32,
+        normed, time_the_levels_all(local_cols, 1), preferred_element_type=jnp.float32
     ).astype(jnp.bfloat16)
     return passed_along(mixed_rows[None], "section", 1)
 

time: 529 us -> 512 us (0.968)
  the two profiles are of different devices: /device:TPU:32 before, /device:TPU:8 now
where the time goes in v1:
time: 512 us; the launch traced here: 511 us
  waiting for transfers between devices  187 us (37%)
  other arithmetic  167 us (33%)
  starting transfers between devices  60.5 us (12%)
  matrix products  53.4 us (10%)
  local copies, waits for them, and re-layouts  27.7 us (5%)
  between operations  14.4 us (3%)
    another operation x2, other arithmetic, span_terms(): jax.scipy.linalg.solve_triangular(unit_lower, right_sides, lower=True, un...  158 us
    all_gather x2, waiting for transfers between devices, entering(): pieces = jax.tree.map(lambda part: lax.all_gather(part, axis), value)  125 us
    ppermute x8, waiting for transfers between devices, time_the_levels_all(): lax.ppermute(taken_in, dev_axis, [(dev_j, (dev_j + 1) % val2) for dev_j i...  47.5 us
    ppermute x7, starting transfers between devices, time_the_levels_all(): lax.ppermute(e_next, dev_axis, [(dev_j, (dev_j - 1) % val2) for dev_j in...  37.2 us
    dot_general x15, matrix products, combine_pairs(): jnp.einsum('hde,hef->hdf', second_map, first_add, precision=highest)  28.1 us
    ppermute x8, starting transfers between devices, time_the_levels_all(): lax.ppermute(taken_in, dev_axis, [(dev_j, (dev_j + 1) % val2) for dev_j i...  17.6 us
    ppermute x1, waiting for transfers between devices, passed_along(): return lax.ppermute(value, axis, pairs)  10.7 us
  transfers between devices with their start and end apart: 19, of which 15 were waited for; matrix products, arithmetic and copies ran while one was open for 5% of the time, Pallas kernels for 0%

profile of v1, /device:TPU:8, one launch (start us, length us, event | category | flops | bytes accessed | tf_op | source)
XLA Modules:
  0.0 510.5 jit_solution(17492314483921267301)
XLA Ops:
  7.6 3.8 collective-permute-start
  22.1 2.4 fusion.36
  24.5 157.9 %custom-call.4 = f32[8,2,1,128,128]{3,4,2,1,0:T(8,128)} custom-call(f32[8,2,1,128,128]{4,3,2,1,0:T(8,128)S(1)} %fusion.36), custom_call_target="InvertDiagBlocksLowerTriangular" | custom-call | tf_op jit(solution)/shard_map/jit(_solve_triangular)/vmap(vmap())/triangular_solve | solution.py:128
  182.4 1.9 broadcast_multiply_fusion
  184.3 2.0 fusion.28
  186.3 2.2 convolution_bitcast_fusion
  188.5 2.2 fusion.32
  191.0 2.8 while.40
  195.5 3.8 collective-permute-start.1
  199.3 7.3 %collective-permute-start.2 = (bf16[1024,128]{1,0:T(8,128)(2,1)S(1)}, bf16[1024,128]{1,0:T(8,128)(2,1)}, u32[]{:S(2)}, u32[]{:S(2)}) collective-permute-start(bf16[1024,128]{1,0:T(8,128)(2,1)S(1)} %bitcast.169), channel_id=1, source_target_pairs={{0,15},{1,0},{2,1},{3,2},{4,3},{5,4},{6,5},{7,6},{8,7},{9,8},{10,9... | collective-permute-start | bytes 786440 | tf_op jit(solution)/shard_map/ppermute | solution.py:32
  207.3 2.5 broadcast_in_dim.67
  212.4 2.1 collective-permute-start.3
  214.5 2.1 convolution_multiply_fusion.1
  216.6 5.1 %collective-permute-start.4 = (bf16[1024,128]{1,0:T(8,128)(2,1)}, bf16[1024,128]{1,0:T(8,128)(2,1)S(1)}, u32[]{:S(2)}, u32[]{:S(2)}) collective-permute-start(bf16[1024,128]{1,0:T(8,128)(2,1)} %collective-permute-done.2), channel_id=1, source_target_pairs={{0,15},{1,0},{2,1},{3,2},{4,3},{5,4},{6,5},{7,6},{8,7},{9,8},{10,9... | collective-permute-start | bytes 786440 | tf_op jit(solution)/shard_map/ppermute | solution.py:32
  221.8 6.9 %collective-permute-done.3 = bf16[1024,128]{1,0:T(8,128)(2,1)S(1)} collective-permute-done((bf16[1024,128]{1,0:T(8,128)(2,1)S(1)}, bf16[1024,128]{1,0:T(8,128)(2,1)S(1)}, u32[]{:S(2)}, u32[]{:S(2)}) %collective-permute-start.3) | collective-permute-done | bytes 262176 | tf_op jit(solution)/shard_map/ppermute | solution.py:25
  228.6 2.1 collective-permute-start.5
  233.0 4.8 collective-permute-start.6
  237.7 7.0 %collective-permute-done.5 = bf16[1024,128]{1,0:T(8,128)(2,1)S(1)} collective-permute-done((bf16[1024,128]{1,0:T(8,128)(2,1)S(1)}, bf16[1024,128]{1,0:T(8,128)(2,1)S(1)}, u32[]{:S(2)}, u32[]{:S(2)}) %collective-permute-start.5) | collective-permute-done | bytes 262176 | tf_op jit(solution)/shard_map/ppermute | solution.py:25
  244.7 1.9 collective-permute-start.7
  246.6 1.9 convolution_bitcast_fusion.2
  249.3 5.1 %collective-permute-start.8 = (bf16[1024,128]{1,0:T(8,128)(2,1)S(1)}, bf16[1024,128]{1,0:T(8,128)(2,1)S(1)}, u32[]{:S(2)}, u32[]{:S(2)}) collective-permute-start(bf16[1024,128]{1,0:T(8,128)(2,1)S(1)} %collective-permute-done.6), channel_id=1, source_target_pairs={{0,15},{1,0},{2,1},{3,2},{4,3},{5,4},{6,5},{7,6},{8,7},{9,8},{10,9... | collective-permute-start | bytes 786440 | tf_op jit(solution)/shard_map/ppermute | solution.py:32
  256.1 4.5 collective-permute-done.7
  260.6 1.9 collective-permute-start.9
  264.9 5.0 collective-permute-start.10
  270.7 5.9 %collective-permute-done.9 = bf16[1024,128]{1,0:T(8,128)(2,1)S(1)} collective-permute-done((bf16[1024,128]{1,0:T(8,128)(2,1)S(1)}, bf16[1024,128]{1,0:T(8,128)(2,1)S(1)}, u32[]{:S(2)}, u32[]{:S(2)}) %collective-permute-start.9) | collective-permute-done | bytes 262176 | tf_op jit(solution)/shard_map/ppermute | solution.py:25
  276.6 1.9 collective-permute-start.11
  280.3 5.1 %collective-permute-start.12 = (bf16[1024,128]{1,0:T(8,128)(2,1)S(1)}, bf16[1024,128]{1,0:T(8,128)(2,1)S(1)}, u32[]{:S(2)}, u32[]{:S(2)}) collective-permute-start(bf16[1024,128]{1,0:T(8,128)(2,1)S(1)} %collective-permute-done.10), channel_id=1, source_target_pairs={{0,15},{1,0},{2,1},{3,2},{4,3},{5,4},{6,5},{7,6},{8,7},{9,8},{10,9... | collective-permute-start | bytes 786440 | tf_op jit(solution)/shard_map/ppermute | solution.py:32
  286.2 6.3 %collective-permute-done.11 = bf16[1024,128]{1,0:T(8,128)(2,1)S(1)} collective-permute-done((bf16[1024,128]{1,0:T(8,128)(2,1)S(1)}, bf16[1024,128]{1,0:T(8,128)(2,1)S(1)}, u32[]{:S(2)}, u32[]{:S(2)}) %collective-permute-start.11) | collective-permute-done | bytes 262176 | tf_op jit(solution)/shard_map/ppermute | solution.py:25
  292.5 1.9 collective-permute-start.13
  296.3 4.7 collective-permute-start.14
  301.8 6.6 %collective-permute-done.13 = bf16[1024,128]{1,0:T(8,128)(2,1)S(1)} collective-permute-done((bf16[1024,128]{1,0:T(8,128)(2,1)S(1)}, bf16[1024,128]{1,0:T(8,128)(2,1)S(1)}, u32[]{:S(2)}, u32[]{:S(2)}) %collective-permute-start.13) | collective-permute-done | bytes 262176 | tf_op jit(solution)/shard_map/ppermute | solution.py:25
  308.4 1.9 collective-permute-start.15
  313.2 10.4 %collective-permute-done.15 = bf16[1024,128]{1,0:T(8,128)(2,1)S(1)} collective-permute-done((bf16[1024,128]{1,0:T(8,128)(2,1)S(1)}, bf16[1024,128]{1,0:T(8,128)(2,1)S(1)}, u32[]{:S(2)}, u32[]{:S(2)}) %collective-permute-start.15) | collective-permute-done | bytes 262176 | tf_op jit(solution)/shard_map/ppermute | solution.py:25
  324.4 17.6 %all-gather.7.cloned.1.call-done = f32[128,128,128]{2,1,0:T(8,128)} async-done(((f32[8,128,128]{2,1,0:T(8,128)}), f32[128,128,128]{2,1,0:T(8,128)}) %all-gather.7.cloned.1.call-update) | async-done | bytes 8388624 | tf_op jit(solution)/shard_map/all_gather | solution.py:49
  342.0 107.2 %all-gather.5.cloned.1.call-done = f32[128,128,128]{2,1,0:T(8,128)} async-done(((f32[8,128,128]{2,1,0:T(8,128)}), f32[128,128,128]{2,1,0:T(8,128)}) %all-gather.5.cloned.1.call-update) | async-done | bytes 8388624 | tf_op jit(solution)/shard_map/all_gather | solution.py:49
  449.2 29.2 %while.41 = (s32[]{:T(128)}, f32[8,128,128]{2,1,0:T(8,128)S(1)}, s32[]{:T(128)}, f32[16,8,128,128]{3,2,1,0:T(8,128)}, f32[16,8,128,128]{3,2,1,0:T(8,128)}, /*index=5*/s32[]{:T(128)}, s32[]{:T(128)}) while((s32[]{:T(128)}, f32[8,128,128]{2,1,0:T(8,128)S(1)}, s32[]{:T(128)}, f32[16,8,128,128]{3,2,1,0:T(8,128)}, ...), condition=%wide.region_5.6_spmd.clone, body=%wide.region_4.5_spmd.clone.sunk | while | flops 201850880 | bytes 3672679 | solution.py:58
  449.2 1.9 fusion.91
  453.1 1.9 fusion.91
  455.0 1.9 fusion.91
  457.0 1.9 fusion.91
  458.9 1.9 fusion.91
  470.6 1.9 fusion.91
  478.4 6.0 %while.39 = (s32[]{:T(128)}, f32[8,128,128]{2,1,0:T(8,128)S(1)}, f32[2,8,64,128]{3,2,1,0:T(8,128)}, f32[2,8,128,128]{3,2,1,0:T(8,128)S(1)}, f32[2,8,128,128]{3,2...) while((s32[]{:T(128)}, f32[8,128,128]{2,1,0:T(8,128)S(1)}, ...), condition=%wide.region_8.9_spmd, body=%wide.region_7.8_spmd.sunk | while | flops 302186496 | bytes 4458589 | solution.py:199
  478.4 2.3 fusion.83
  481.4 2.3 fusion.83
  487.3 3.0 fusion.27
  490.3 1.9 collective-permute-start.16
  492.2 10.7 %collective-permute-done.16 = bf16[1,128,2048]{2,1,0:T(8,128)(2,1)S(1)} collective-permute-done((bf16[1,128,2048]{2,1,0:T(8,128)(2,1)S(1)}, bf16[1,128,2048]{2,1,0:T(8,128)(2,1)S(1)}, u32[]{:S(2)}, u32[]{:S(2)}) %collective-permute-start.16) | collective-permute-done | bytes 524320 | tf_op jit(solution)/shard_map/ppermute | solution.py:64
  (149 shorter events, 58.1 us)
Async XLA Ops:
  6.5 9.1 %copy-start.7 = (bf16[1,128,5120]{2,1,0:T(8,128)(2,1)S(1)}, bf16[1,128,5120]{2,1,0:T(8,128)(2,1)}, u32[]{:S(2)}) copy-start(bf16[1,128,5120]{2,1,0:T(8,128)(2,1)} %param.12) | copy-start | bytes 3932164
  6.5 335.4 %all-gather.7.cloned.1.call-start = ((), (), s32[]{:S(2)}) async-start(), calls=%async_computation.1 | async-start | bytes 8912896 | tf_op jit(solution)/shard_map/all_gather | solution.py:49
  7.6 8.1 %collective-permute-start = (bf16[3,5120]{1,0:T(4,128)(2,1)S(1)}, bf16[3,5120]{1,0:T(4,128)(2,1)S(1)}, u32[]{:S(2)}, u32[]{:S(2)}) collective-permute-start(bf16[3,5120]{1,0:T(4,128)(2,1)S(1)} %slice_bitcast_fusion.3), channel_id=1, source_target_pairs={{0,1},{1,2},{2,3},{3,4},{4,5},{5,6},{6,7},{7,8},{8,9},{9,10},{10,1... | collective-permute-start | bytes 92168 | tf_op jit(solution)/shard_map/ppermute | solution.py:44
  17.5 1.5 copy-start.6
  22.1 166.4 %copy-start = (f32[8,128,2,128]{3,2,1,0:T(2,128)}, f32[8,128,2,128]{3,2,1,0:T(2,128)S(1)}, u32[]{:S(2)}) copy-start(f32[8,128,2,128]{3,2,1,0:T(2,128)S(1)} %copy.83) | copy-start | bytes 3145732
  182.4 1.9 copy-start.8
  186.3 4.5 copy-start.3
  191.0 4.4 copy-start.9
  193.8 0.8 copy-start.5
  193.9 1.0 copy-start.2
  194.7 254.5 %all-gather.5.cloned.1.call-start = ((), (), s32[]{:S(2)}) async-start(), calls=%async_computation | async-start | bytes 8912896 | tf_op jit(solution)/shard_map/all_gather | solution.py:49
  195.5 16.9 %collective-permute-start.1 = (bf16[1024,128]{1,0:T(8,128)(2,1)S(1)}, bf16[1024,128]{1,0:T(8,128)(2,1)S(1)}, u32[]{:S(2)}, u32[]{:S(2)}) collective-permute-start(bf16[1024,128]{1,0:T(8,128)(2,1)S(1)} %bitcast.168), channel_id=1, source_target_pairs={{0,1},{1,2},{2,3},{3,4},{4,5},{5,6},{6,7},{7,8},{8,9},{9,10},{10,1... | collective-permute-start | bytes 786440 | tf_op jit(solution)/shard_map/ppermute | solution.py:25
  199.3 17.3 %collective-permute-start.2 = (bf16[1024,128]{1,0:T(8,128)(2,1)S(1)}, bf16[1024,128]{1,0:T(8,128)(2,1)}, u32[]{:S(2)}, u32[]{:S(2)}) collective-permute-start(bf16[1024,128]{1,0:T(8,128)(2,1)S(1)} %bitcast.169), channel_id=1, source_target_pairs={{0,15},{1,0},{2,1},{3,2},{4,3},{5,4},{6,5},{7,6},{8,7},{9,8},{10,9... | collective-permute-start | bytes 786440 | tf_op jit(solution)/shard_map/ppermute | solution.py:32
  210.5 3.9 copy-start.1
  211.8 19.0 %copy-start.4 = (f32[8,2,128,256]{3,2,1,0:T(8,128)S(1)}, f32[8,2,128,256]{3,2,1,0:T(8,128)}, u32[]{:S(2)}) copy-start(f32[8,2,128,256]{3,2,1,0:T(8,128)} %copy-done.3) | copy-start | bytes 6291460
  212.4 16.2 %copy-start.10 = (bf16[1024,128]{1,0:T(8,128)(2,1)}, bf16[1024,128]{1,0:T(8,128)(2,1)S(1)}, u32[]{:S(2)}) copy-start(bf16[1024,128]{1,0:T(8,128)(2,1)S(1)} %collective-permute-done.1) | copy-start | bytes 786436
  212.4 16.2 %collective-permute-start.3 = (bf16[1024,128]{1,0:T(8,128)(2,1)S(1)}, bf16[1024,128]{1,0:T(8,128)(2,1)S(1)}, u32[]{:S(2)}, u32[]{:S(2)}) collective-permute-start(bf16[1024,128]{1,0:T(8,128)(2,1)S(1)} %collective-permute-done.1), channel_id=1, source_target_pairs={{0,1},{1,2},{2,3},{3,4},{4,5},{5,6},{6,7},{7,8},{8,9},{9,10},{10,1... | collective-permute-start | bytes 786440 | tf_op jit(solution)/shard_map/ppermute | solution.py:25
  216.6 16.4 %collective-permute-start.4 = (bf16[1024,128]{1,0:T(8,128)(2,1)}, bf16[1024,128]{1,0:T(8,128)(2,1)S(1)}, u32[]{:S(2)}, u32[]{:S(2)}) collective-permute-start(bf16[1024,128]{1,0:T(8,128)(2,1)} %collective-permute-done.2), channel_id=1, source_target_pairs={{0,15},{1,0},{2,1},{3,2},{4,3},{5,4},{6,5},{7,6},{8,7},{9,8},{10,9... | collective-permute-start | bytes 786440 | tf_op jit(solution)/shard_map/ppermute | solution.py:32
  228.6 16.1 %collective-permute-start.5 = (bf16[1024,128]{1,0:T(8,128)(2,1)S(1)}, bf16[1024,128]{1,0:T(8,128)(2,1)S(1)}, u32[]{:S(2)}, u32[]{:S(2)}) collective-permute-start(bf16[1024,128]{1,0:T(8,128)(2,1)S(1)} %collective-permute-done.3), channel_id=1, source_target_pairs={{0,1},{1,2},{2,3},{3,4},{4,5},{5,6},{6,7},{7,8},{8,9},{9,10},{10,1... | collective-permute-start | bytes 786440 | tf_op jit(solution)/shard_map/ppermute | solution.py:25
  230.8 17.8 %copy-start.11 = (bf16[1024,128]{1,0:T(8,128)(2,1)S(1)}, bf16[1024,128]{1,0:T(8,128)(2,1)}, u32[]{:S(2)}) copy-start(bf16[1024,128]{1,0:T(8,128)(2,1)} %copy-done.10) | copy-start | bytes 786436
  233.0 16.3 %collective-permute-start.6 = (bf16[1024,128]{1,0:T(8,128)(2,1)S(1)}, bf16[1024,128]{1,0:T(8,128)(2,1)S(1)}, u32[]{:S(2)}, u32[]{:S(2)}) collective-permute-start(bf16[1024,128]{1,0:T(8,128)(2,1)S(1)} %collective-permute-done.4), channel_id=1, source_target_pairs={{0,15},{1,0},{2,1},{3,2},{4,3},{5,4},{6,5},{7,6},{8,7},{9,8},{10,9... | collective-permute-start | bytes 786440 | tf_op jit(solution)/shard_map/ppermute | solution.py:32
  244.7 15.9 %collective-permute-start.7 = (bf16[1024,128]{1,0:T(8,128)(2,1)S(1)}, bf16[1024,128]{1,0:T(8,128)(2,1)S(1)}, u32[]{:S(2)}, u32[]{:S(2)}) collective-permute-start(bf16[1024,128]{1,0:T(8,128)(2,1)S(1)} %collective-permute-done.5), channel_id=1, source_target_pairs={{0,1},{1,2},{2,3},{3,4},{4,5},{5,6},{6,7},{7,8},{8,9},{9,10},{10,1... | collective-permute-start | bytes 786440 | tf_op jit(solution)/shard_map/ppermute | solution.py:25
  249.3 15.6 %collective-permute-start.8 = (bf16[1024,128]{1,0:T(8,128)(2,1)S(1)}, bf16[1024,128]{1,0:T(8,128)(2,1)S(1)}, u32[]{:S(2)}, u32[]{:S(2)}) collective-permute-start(bf16[1024,128]{1,0:T(8,128)(2,1)S(1)} %collective-permute-done.6), channel_id=1, source_target_pairs={{0,15},{1,0},{2,1},{3,2},{4,3},{5,4},{6,5},{7,6},{8,7},{9,8},{10,9... | collective-permute-start | bytes 786440 | tf_op jit(solution)/shard_map/ppermute | solution.py:32
  260.6 15.9 %collective-permute-start.9 = (bf16[1024,128]{1,0:T(8,128)(2,1)S(1)}, bf16[1024,128]{1,0:T(8,128)(2,1)S(1)}, u32[]{:S(2)}, u32[]{:S(2)}) collective-permute-start(bf16[1024,128]{1,0:T(8,128)(2,1)S(1)} %collective-permute-done.7), channel_id=1, source_target_pairs={{0,1},{1,2},{2,3},{3,4},{4,5},{5,6},{6,7},{7,8},{8,9},{9,10},{10,1... | collective-permute-start | bytes 786440 | tf_op jit(solution)/shard_map/ppermute | solution.py:25
  264.9 15.4 %collective-permute-start.10 = (bf16[1024,128]{1,0:T(8,128)(2,1)S(1)}, bf16[1024,128]{1,0:T(8,128)(2,1)S(1)}, u32[]{:S(2)}, u32[]{:S(2)}) collective-permute-start(bf16[1024,128]{1,0:T(8,128)(2,1)S(1)} %collective-permute-done.8), channel_id=1, source_target_pairs={{0,15},{1,0},{2,1},{3,2},{4,3},{5,4},{6,5},{7,6},{8,7},{9,8},{10,9... | collective-permute-start | bytes 786440 | tf_op jit(solution)/shard_map/ppermute | solution.py:32
  276.6 15.9 %collective-permute-start.11 = (bf16[1024,128]{1,0:T(8,128)(2,1)S(1)}, bf16[1024,128]{1,0:T(8,128)(2,1)S(1)}, u32[]{:S(2)}, u32[]{:S(2)}) collective-permute-start(bf16[1024,128]{1,0:T(8,128)(2,1)S(1)} %collective-permute-done.9), channel_id=1, source_target_pairs={{0,1},{1,2},{2,3},{3,4},{4,5},{5,6},{6,7},{7,8},{8,9},{9,10},{10,1... | collective-permute-start | bytes 786440 | tf_op jit(solution)/shard_map/ppermute | solution.py:25
  280.3 16.0 %collective-permute-start.12 = (bf16[1024,128]{1,0:T(8,128)(2,1)S(1)}, bf16[1024,128]{1,0:T(8,128)(2,1)S(1)}, u32[]{:S(2)}, u32[]{:S(2)}) collective-permute-start(bf16[1024,128]{1,0:T(8,128)(2,1)S(1)} %collective-permute-done.10), channel_id=1, source_target_pairs={{0,15},{1,0},{2,1},{3,2},{4,3},{5,4},{6,5},{7,6},{8,7},{9,8},{10,9... | collective-permute-start | bytes 786440 | tf_op jit(solution)/shard_map/ppermute | solution.py:32
  292.5 15.9 %collective-permute-start.13 = (bf16[1024,128]{1,0:T(8,128)(2,1)S(1)}, bf16[1024,128]{1,0:T(8,128)(2,1)S(1)}, u32[]{:S(2)}, u32[]{:S(2)}) collective-permute-start(bf16[1024,128]{1,0:T(8,128)(2,1)S(1)} %collective-permute-done.11), channel_id=1, source_target_pairs={{0,1},{1,2},{2,3},{3,4},{4,5},{5,6},{6,7},{7,8},{8,9},{9,10},{10,1... | collective-permute-start | bytes 786440 | tf_op jit(solution)/shard_map/ppermute | solution.py:25
  296.3 16.1 %collective-permute-start.14 = (bf16[1024,128]{1,0:T(8,128)(2,1)S(1)}, bf16[1024,128]{1,0:T(8,128)(2,1)S(1)}, u32[]{:S(2)}, u32[]{:S(2)}) collective-permute-start(bf16[1024,128]{1,0:T(8,128)(2,1)S(1)} %collective-permute-done.12), channel_id=1, source_target_pairs={{0,15},{1,0},{2,1},{3,2},{4,3},{5,4},{6,5},{7,6},{8,7},{9,8},{10,9... | collective-permute-start | bytes 786440 | tf_op jit(solution)/shard_map/ppermute | solution.py:32
  308.4 15.2 %collective-permute-start.15 = (bf16[1024,128]{1,0:T(8,128)(2,1)S(1)}, bf16[1024,128]{1,0:T(8,128)(2,1)S(1)}, u32[]{:S(2)}, u32[]{:S(2)}) collective-permute-start(bf16[1024,128]{1,0:T(8,128)(2,1)S(1)} %collective-permute-done.13), channel_id=1, source_target_pairs={{0,1},{1,2},{2,3},{3,4},{4,5},{5,6},{6,7},{7,8},{8,9},{9,10},{10,1... | collective-permute-start | bytes 786440 | tf_op jit(solution)/shard_map/ppermute | solution.py:25
  478.3 8.9 %copy-start.12 = (f32[1,1024]{1,0:T(1,128)S(1)}, f32[1,1024]{1,0:T(1,128)}, u32[]{:S(2)}) copy-start(f32[1,1024]{1,0:T(1,128)} %param.16) | copy-start | bytes 12292
  490.3 12.6 %collective-permute-start.16 = (bf16[1,128,2048]{2,1,0:T(8,128)(2,1)S(1)}, bf16[1,128,2048]{2,1,0:T(8,128)(2,1)S(1)}, u32[]{:S(2)}, u32[]{:S(2)}) collective-permute-start(bf16[1,128,2048]{2,1,0:T(8,128)(2,1)S(1)} %fusion.27), channel_id=1, source_target_pairs={{0,16},{16,32},{32,48},{48,64},{64,80},{80,96},{96,112},{112,128},... | collective-permute-start | bytes 1572872 | tf_op jit(solution)/shard_map/ppermute | solution.py:64
Sparse Core Ops, SparseCore 0:
  194.8 147.0 all-gather.6
  344.0 105.0 all-gather.4
